TPU v7x, 32 devices: a whole 2x2x4 slice. The times are simulated.
32 devices in a mesh: dp: 16 (over z, x, core), tensor: 2 (over y).
Axes of the slice: x: 2, y: 2, z: 4, core: 2. Of those that a mesh axis runs over, the one named last changes fastest.
Arguments:
- tokens: bfloat16 [32768, 768], P(('dp', 'tensor')), may hold values from -6 to 6
- segment_ids: int32 [16, 2048], P('dp'), may hold values from 0 to 15, never falling along the last dimension, each value on 1 to 1024 neighbouring positions
- ln1_gain: bfloat16 [768], P('dp'), may hold values from 0.25 to 1.75
- ln1_bias: bfloat16 [768], P('dp'), may hold values from -1.796875 to 1.796875
- w_qkv: bfloat16 [768, 3, 768], P('dp', None, 'tensor'), may hold values from -0.3125 to 0.3125
- b_qv: bfloat16 [2, 768], P(None, 'dp'), may hold values from -1.796875 to 1.796875
- w_attn_out: bfloat16 [768, 768], P('tensor', 'dp'), may hold values from -3 to 3
- b_attn_out: bfloat16 [768], P('dp'), may hold values from -6 to 6
- ln2_gain: bfloat16 [768], P('dp'), may hold values from 0.25 to 1.75
- ln2_bias: bfloat16 [768], P('dp'), may hold values from -1.796875 to 1.796875
- w_fc: bfloat16 [768, 3072], P('dp', 'tensor'), may hold values from -0.21875 to 0.21875
- b_fc: bfloat16 [3072], P('dp'), may hold values from -1.796875 to 1.796875
- w_proj: bfloat16 [3072, 768], P('tensor', 'dp'), may hold values from -0.8984375 to 0.8984375
- b_proj: bfloat16 [768], P('dp'), may hold values from -6 to 6
- cotangent: bfloat16 [32768, 768], P(('dp', 'tensor')), may hold values from -6 to 6
Outputs:
- block_out: bfloat16 [32768, 768], P(('dp', 'tensor'))
- grad_tokens: bfloat16 [32768, 768], P(('dp', 'tensor'))
- grad_ln1_gain: float32 [768], P('dp')
- grad_ln1_bias: float32 [768], P('dp')
- grad_w_qkv: float32 [768, 3, 768], P('dp', None, 'tensor')
- grad_b_qv: float32 [2, 768], P(None, 'dp')
- grad_w_attn_out: float32 [768, 768], P('tensor', 'dp')
- grad_b_attn_out: float32 [768], P('dp')
- grad_ln2_gain: float32 [768], P('dp')
- grad_ln2_bias: float32 [768], P('dp')
- grad_w_fc: float32 [768, 3072], P('dp', 'tensor')
- grad_b_fc: float32 [3072], P('dp')
- grad_w_proj: float32 [3072, 768], P('tensor', 'dp')
- grad_b_proj: float32 [768], P('dp')
Inputs may be any that keep to these rules, and one draw needn't show every extreme that they name: `segment_ids`: in each sequence the document numbers never fall; each document has 1 to 1024 tokens, and one has exactly 1024.
All inputs are finite; a program needn't handle non-finite values.
Results may differ from a plain program's by a relative error of at most 0.02.
Values may be sent and summed in bfloat16 or wider, within the bound.
A program may use at most 256 MiB of HBM per device.

v0:
```python
import jax
import jax.numpy as jnp
from jax import lax
from jax.sharding import PartitionSpec as P

HEAD_DIM = 64
EPSILON = 1e-05
BRANCH_SCALE = 48.0 ** (-0.5)
MASKED_SCORE = -1e30


def layer_norm(values, gain, offsets):
    centered = values - jnp.mean(values, axis=-1, keepdims=True)
    variance = jnp.mean(centered * centered, axis=-1, keepdims=True)
    return centered * lax.rsqrt(variance + EPSILON) * gain + offsets


def gelu_tanh(values):
    return jax.nn.gelu(values, approximate=True)


def contract_rows(left, right):
    return lax.dot_general(
        left, right, (((0,), (0,)), ((), ())), preferred_element_type=jnp.float32
    )


def contract_cols(left, right):
    return lax.dot_general(
        left, right, (((1,), (1,)), ((), ())), preferred_element_type=jnp.float32
    )


def visible_mask(seg_row, row_start, block_rows):
    seq_len = seg_row.shape[0]
    seg_query = lax.dynamic_slice_in_dim(seg_row, row_start, block_rows, 0)
    query_pos = row_start + jnp.arange(block_rows, dtype=jnp.int32)
    key_pos = jnp.arange(seq_len, dtype=jnp.int32)
    return (seg_query[:, None] == seg_row[None, :]) & (query_pos[:, None] >= key_pos[None, :])


def on_device(
    tokens,
    segment_ids,
    ln1_gain,
    ln1_bias,
    w_qkv,
    b_qv,
    w_attn_out,
    b_attn_out,
    ln2_gain,
    ln2_bias,
    w_fc,
    b_fc,
    w_proj,
    b_proj,
    cotangent,
):
    model_width = tokens.shape[1]
    local_rows = tokens.shape[0]
    local_cols = w_qkv.shape[2]
    hidden_cols = w_fc.shape[1]
    heads_here = local_cols // HEAD_DIM
    seg_row = segment_ids[0]
    seq_len = seg_row.shape[0]
    score_scale = HEAD_DIM ** (-0.5)
    tensor_pos = lax.axis_index("tensor")
    gain_attn, offset_attn, qkv_weight, qv_bias_all, out_weight, out_bias = (
        lax.all_gather(ln1_gain, "dp", axis=0, tiled=True),
        lax.all_gather(ln1_bias, "dp", axis=0, tiled=True),
        lax.all_gather(w_qkv, "dp", axis=0, tiled=True),
        lax.all_gather(b_qv, "dp", axis=1, tiled=True),
        lax.all_gather(w_attn_out, "dp", axis=1, tiled=True),
        lax.all_gather(b_attn_out, "dp", axis=0, tiled=True),
    )
    qkv_flat_weight = qkv_weight.reshape(model_width, 3 * local_cols)
    qv_bias = lax.dynamic_slice_in_dim(qv_bias_all, tensor_pos * local_cols, local_cols, 1).astype(
        jnp.float32
    )
    qkv_bias = jnp.stack([qv_bias[0], jnp.zeros((local_cols,), jnp.float32), qv_bias[1]])
    residual_in = tokens.astype(jnp.float32)
    normed_one = layer_norm(
        residual_in, gain_attn.astype(jnp.float32), offset_attn.astype(jnp.float32)
    ).astype(jnp.bfloat16)
    full_one = lax.all_gather(normed_one, "tensor", axis=0, tiled=True)
    projected = (
        jnp.dot(full_one, qkv_flat_weight, preferred_element_type=jnp.float32).reshape(
            seq_len, 3, local_cols
        )
        + qkv_bias
    ).astype(jnp.bfloat16)
    queries = projected[:, 0]
    keys_all = projected[:, 1]
    values_all = projected[:, 2]
    block_rows = min(512, seq_len)
    starts = jnp.arange(seq_len // block_rows, dtype=jnp.int32) * block_rows

    def forward_block(row_start):
        visible = visible_mask(seg_row, row_start, block_rows)
        query_block = lax.dynamic_slice_in_dim(queries, row_start, block_rows, 0)
        pieces = []
        logsums = []
        for head_index in range(heads_here):
            low_col = head_index * HEAD_DIM
            high_col = low_col + HEAD_DIM
            raw_scores = contract_cols(
                query_block[:, low_col:high_col], keys_all[:, low_col:high_col]
            )
            scores = jnp.where(visible, raw_scores * score_scale, MASKED_SCORE)
            row_max = jnp.max(scores, axis=1, keepdims=True)
            exponent = jnp.exp(scores - row_max)
            row_total = jnp.sum(exponent, axis=1, keepdims=True)
            soft_weights = (exponent / row_total).astype(jnp.bfloat16)
            pieces.append(
                jnp.dot(
                    soft_weights,
                    values_all[:, low_col:high_col],
                    preferred_element_type=jnp.float32,
                )
            )
            logsums.append(row_max[:, 0] + jnp.log(row_total[:, 0]))
        return (jnp.concatenate(pieces, axis=1).astype(jnp.bfloat16), jnp.stack(logsums))

    attn_blocks, logsum_blocks = lax.map(forward_block, starts)
    attended = attn_blocks.reshape(seq_len, local_cols)
    attn_branch = lax.psum_scatter(
        jnp.dot(
            lax.slice_in_dim(attended, 0, lax.axis_size("tensor") * local_rows, axis=0),
            out_weight,
            preferred_element_type=jnp.float32,
        ).astype(jnp.bfloat16),
        "tensor",
        scatter_dimension=0,
        tiled=True,
    ).astype(jnp.float32) + out_bias.astype(jnp.float32)
    middle = residual_in + BRANCH_SCALE * attn_branch
    gain_mlp, offset_mlp, fc_weight, fc_bias_all, proj_weight, proj_bias = (
        lax.all_gather(ln2_gain, "dp", axis=0, tiled=True),
        lax.all_gather(ln2_bias, "dp", axis=0, tiled=True),
        lax.all_gather(w_fc, "dp", axis=0, tiled=True),
        lax.all_gather(b_fc, "dp", axis=0, tiled=True),
        lax.all_gather(w_proj, "dp", axis=1, tiled=True),
        lax.all_gather(b_proj, "dp", axis=0, tiled=True),
    )
    fc_bias = lax.dynamic_slice_in_dim(
        fc_bias_all, tensor_pos * hidden_cols, hidden_cols, 0
    ).astype(jnp.float32)
    normed_two = layer_norm(
        middle, gain_mlp.astype(jnp.float32), offset_mlp.astype(jnp.float32)
    ).astype(jnp.bfloat16)
    full_two = lax.all_gather(normed_two, "tensor", axis=0, tiled=True)
    inputs_rows = lax.slice_in_dim(full_two, 0, lax.axis_size("tensor") * local_rows, axis=0)
    activated = gelu_tanh(
        jnp.dot(inputs_rows, fc_weight, preferred_element_type=jnp.float32) + fc_bias
    ).astype(jnp.bfloat16)
    mlp_branch = lax.psum_scatter(
        jnp.dot(activated, proj_weight, preferred_element_type=jnp.float32).astype(jnp.bfloat16),
        "tensor",
        scatter_dimension=0,
        tiled=True,
    ).astype(jnp.float32) + proj_bias.astype(jnp.float32)
    block_out = (middle + BRANCH_SCALE * mlp_branch).astype(jnp.bfloat16)
    (
        gain_attn,
        offset_attn,
        qkv_weight,
        out_weight,
        gain_mlp,
        offset_mlp,
        fc_weight,
        fc_bias_all,
        proj_weight,
    ) = (
        lax.all_gather(ln1_gain, "dp", axis=0, tiled=True),
        lax.all_gather(ln1_bias, "dp", axis=0, tiled=True),
        lax.all_gather(w_qkv, "dp", axis=0, tiled=True),
        lax.all_gather(w_attn_out, "dp", axis=1, tiled=True),
        lax.all_gather(ln2_gain, "dp", axis=0, tiled=True),
        lax.all_gather(ln2_bias, "dp", axis=0, tiled=True),
        lax.all_gather(w_fc, "dp", axis=0, tiled=True),
        lax.all_gather(b_fc, "dp", axis=0, tiled=True),
        lax.all_gather(w_proj, "dp", axis=1, tiled=True),
    )
    qkv_flat_weight = qkv_weight.reshape(model_width, 3 * local_cols)
    fc_bias = lax.dynamic_slice_in_dim(
        fc_bias_all, tensor_pos * hidden_cols, hidden_cols, 0
    ).astype(jnp.float32)
    grad_out = cotangent.astype(jnp.float32)
    scaled_out = BRANCH_SCALE * grad_out
    d_proj_bias = jnp.sum(scaled_out, axis=0)
    d_mlp_full = lax.all_gather(scaled_out.astype(jnp.bfloat16), "tensor", axis=0, tiled=True)
    mlp_block = min(1024, seq_len)

    def mlp_back_block(row_start):
        inputs_rows = lax.dynamic_slice_in_dim(full_two, row_start, mlp_block, 0)
        grad_rows = lax.dynamic_slice_in_dim(d_mlp_full, row_start, mlp_block, 0)
        pre_act = jnp.dot(inputs_rows, fc_weight, preferred_element_type=jnp.float32) + fc_bias
        activated, gelu_back = jax.vjp(gelu_tanh, pre_act)
        d_act = contract_cols(grad_rows, proj_weight)
        d_pre = gelu_back(d_act)[0]
        return (activated.astype(jnp.bfloat16), d_pre.astype(jnp.bfloat16), jnp.sum(d_pre, axis=0))

    act_blocks, dpre_blocks, dbias_blocks = lax.map(
        mlp_back_block, jnp.arange(seq_len // mlp_block, dtype=jnp.int32) * mlp_block
    )
    act_all = act_blocks.reshape(seq_len, hidden_cols)
    d_pre_all = dpre_blocks.reshape(seq_len, hidden_cols)
    d_fc_bias = jnp.sum(dbias_blocks, axis=0)
    d_proj_w = contract_rows(act_all, d_mlp_full)
    d_fc_w = contract_rows(full_two, d_pre_all)
    grad_w_fc, grad_w_proj = (
        lax.psum_scatter(d_fc_w, "dp", scatter_dimension=0, tiled=True),
        lax.psum_scatter(d_proj_w, "dp", scatter_dimension=1, tiled=True),
    )
    d_normed_two = lax.psum_scatter(
        contract_cols(
            lax.slice_in_dim(d_pre_all, 0, lax.axis_size("tensor") * local_rows, axis=0), fc_weight
        ).astype(jnp.bfloat16),
        "tensor",
        scatter_dimension=0,
        tiled=True,
    ).astype(jnp.float32)
    unused_two, norm_back_two = jax.vjp(
        layer_norm, middle, gain_mlp.astype(jnp.float32), offset_mlp.astype(jnp.float32)
    )
    d_middle_part, d_gain_mlp, d_offset_mlp = norm_back_two(d_normed_two)
    d_middle = grad_out + d_middle_part
    scaled_mid = BRANCH_SCALE * d_middle
    d_out_bias = jnp.sum(scaled_mid, axis=0)
    d_attn_full = lax.all_gather(scaled_mid.astype(jnp.bfloat16), "tensor", axis=0, tiled=True)
    d_out_w = contract_rows(attended, d_attn_full)
    d_attended = contract_cols(d_attn_full, out_weight).astype(jnp.bfloat16)

    def backward_block(carry, inputs):
        d_keys_acc, d_values_acc = carry
        row_start, logsum = inputs
        visible = visible_mask(seg_row, row_start, block_rows)
        query_block = lax.dynamic_slice_in_dim(queries, row_start, block_rows, 0)
        grad_block = lax.dynamic_slice_in_dim(d_attended, row_start, block_rows, 0)
        dq_pieces = []
        dk_pieces = []
        dv_pieces = []
        for head_index in range(heads_here):
            low_col = head_index * HEAD_DIM
            high_col = low_col + HEAD_DIM
            query_head = query_block[:, low_col:high_col]
            key_head = keys_all[:, low_col:high_col]
            grad_head = grad_block[:, low_col:high_col]
            raw_scores = contract_cols(query_head, key_head)
            scores = jnp.where(visible, raw_scores * score_scale, MASKED_SCORE)
            soft_weights = jnp.exp(scores - logsum[head_index][:, None])
            d_soft = contract_cols(grad_head, values_all[:, low_col:high_col])
            d_scores = soft_weights * (
                d_soft - jnp.sum(soft_weights * d_soft, axis=1, keepdims=True)
            )
            d_raw = (d_scores * score_scale).astype(jnp.bfloat16)
            dq_pieces.append(jnp.dot(d_raw, key_head, preferred_element_type=jnp.float32))
            dk_pieces.append(contract_rows(d_raw, query_head))
            dv_pieces.append(contract_rows(soft_weights.astype(jnp.bfloat16), grad_head))
        new_carry = (
            d_keys_acc + jnp.concatenate(dk_pieces, axis=1),
            d_values_acc + jnp.concatenate(dv_pieces, axis=1),
        )
        return (new_carry, jnp.concatenate(dq_pieces, axis=1))

    zero_acc = jnp.zeros((seq_len, local_cols), jnp.float32)
    (d_keys, d_values), dq_blocks = lax.scan(
        backward_block, (zero_acc, zero_acc), (starts, logsum_blocks)
    )
    d_queries = dq_blocks.reshape(seq_len, local_cols)
    d_projected = jnp.stack([d_queries, d_keys, d_values], axis=1).astype(jnp.bfloat16)
    part_sums = jnp.sum(d_projected, axis=0, dtype=jnp.float32)
    d_qv_bias = lax.dynamic_update_slice(
        jnp.zeros((2, model_width), jnp.float32),
        jnp.stack([part_sums[0], part_sums[2]]),
        (0, tensor_pos * local_cols),
    )
    d_flat = d_projected.reshape(seq_len, 3 * local_cols)
    d_qkv_w = contract_rows(full_one, d_flat).reshape(model_width, 3, local_cols)
    d_normed_one = lax.psum_scatter(
        contract_cols(d_flat, qkv_flat_weight).astype(jnp.bfloat16),
        "tensor",
        scatter_dimension=0,
        tiled=True,
    ).astype(jnp.float32)
    unused_one, norm_back_one = jax.vjp(
        layer_norm, residual_in, gain_attn.astype(jnp.float32), offset_attn.astype(jnp.float32)
    )
    d_input_part, d_gain_attn, d_offset_attn = norm_back_one(d_normed_one)
    grad_tokens = (d_middle + d_input_part).astype(jnp.bfloat16)
    d_fc_bias_full = lax.dynamic_update_slice(
        jnp.zeros((fc_bias_all.shape[0],), jnp.float32), d_fc_bias, (tensor_pos * hidden_cols,)
    )
    (
        sum_gain_attn,
        sum_offset_attn,
        sum_qv_bias,
        sum_out_bias,
        sum_gain_mlp,
        sum_offset_mlp,
        sum_fc_bias,
        sum_proj_bias,
    ) = (
        lax.psum(d_gain_attn.astype(jnp.bfloat16), "tensor").astype(jnp.float32),
        lax.psum(d_offset_attn.astype(jnp.bfloat16), "tensor").astype(jnp.float32),
        lax.psum(d_qv_bias.astype(jnp.bfloat16), "tensor").astype(jnp.float32),
        lax.psum(d_out_bias.astype(jnp.bfloat16), "tensor").astype(jnp.float32),
        lax.psum(d_gain_mlp.astype(jnp.bfloat16), "tensor").astype(jnp.float32),
        lax.psum(d_offset_mlp.astype(jnp.bfloat16), "tensor").astype(jnp.float32),
        lax.psum(d_fc_bias_full.astype(jnp.bfloat16), "tensor").astype(jnp.float32),
        lax.psum(d_proj_bias.astype(jnp.bfloat16), "tensor").astype(jnp.float32),
    )
    (
        grad_w_qkv,
        grad_w_attn_out,
        grad_ln1_gain,
        grad_ln1_bias,
        grad_b_qv,
        grad_b_attn_out,
        grad_ln2_gain,
        grad_ln2_bias,
        grad_b_fc,
        grad_b_proj,
    ) = (
        lax.psum_scatter(d_qkv_w, "dp", scatter_dimension=0, tiled=True),
        lax.psum_scatter(d_out_w, "dp", scatter_dimension=1, tiled=True),
        lax.psum_scatter(sum_gain_attn, "dp", scatter_dimension=0, tiled=True),
        lax.psum_scatter(sum_offset_attn, "dp", scatter_dimension=0, tiled=True),
        lax.psum_scatter(sum_qv_bias, "dp", scatter_dimension=1, tiled=True),
        lax.psum_scatter(sum_out_bias, "dp", scatter_dimension=0, tiled=True),
        lax.psum_scatter(sum_gain_mlp, "dp", scatter_dimension=0, tiled=True),
        lax.psum_scatter(sum_offset_mlp, "dp", scatter_dimension=0, tiled=True),
        lax.psum_scatter(sum_fc_bias, "dp", scatter_dimension=0, tiled=True),
        lax.psum_scatter(sum_proj_bias, "dp", scatter_dimension=0, tiled=True),
    )
    return (
        block_out,
        grad_tokens,
        grad_ln1_gain,
        grad_ln1_bias,
        grad_w_qkv,
        grad_b_qv,
        grad_w_attn_out,
        grad_b_attn_out,
        grad_ln2_gain,
        grad_ln2_bias,
        grad_w_fc,
        grad_b_fc,
        grad_w_proj,
        grad_b_proj,
    )


def solution(mesh):
    in_specs = (
        P(("dp", "tensor"), None),
        P("dp", None),
        P("dp"),
        P("dp"),
        P("dp", None, "tensor"),
        P(None, "dp"),
        P("tensor", "dp"),
        P("dp"),
        P("dp"),
        P("dp"),
        P("dp", "tensor"),
        P("dp"),
        P("tensor", "dp"),
        P("dp"),
        P(("dp", "tensor"), None),
    )
    out_specs = (
        P(("dp", "tensor"), None),
        P(("dp", "tensor"), None),
        P("dp"),
        P("dp"),
        P("dp", None, "tensor"),
        P(None, "dp"),
        P("tensor", "dp"),
        P("dp"),
        P("dp"),
        P("dp"),
        P("dp", "tensor"),
        P("dp"),
        P("tensor", "dp"),
        P("dp"),
    )
    return jax.shard_map(
        on_device, mesh=mesh, in_specs=in_specs, out_specs=out_specs, check_vma=False
    )
```

profile of v0, /device:TPU:0, one launch (start us, length us, event | category | flops | bytes accessed | tf_op | source)
XLA Modules:
  0.0 1494.2 jit_solution(269349831955712147)
XLA Ops:
  16.5 63.2 %all-reduce.15 = (bf16[768]{0:T(1024)(128)(2,1)}, bf16[768]{0:T(1024)(128)(2,1)}, bf16[768]{0:T(1024)(128)(2,1)}, bf16[768]{0:T(1024)(128)(2,1)S(1)}, bf16[768]{...) all-reduce(bf16[768]{0:T(1024)(128)(2,1)S(1)} %dynamic-update-slice, ...), channel_id=1, replica_groups=mesh['dp'=16,'tensor'=2] {'dp'}, use_global_device_ids=true, to_apply=%add.4 | all-reduce | flops 7680 | bytes 30720
  86.6 17.0 %all-gather = bf16[16,48,2]{1,2,0:T(2,128)(2,1)S(1)} all-gather(bf16[1,48,2]{1,2,0:T(2,128)(2,1)S(1)} %bitcast.226), channel_id=1, replica_groups=mesh['dp'=16,'tensor'=2] {'dp'}, dimensions={0}, use_global_device_ids=true | all-gather | bytes 3264 | tf_op jit(solution)/shard_map/all_gather | solution.py:72
  104.4 22.1 %all_gather.60 = bf16[384,768]{0,1:T(8,128)(2,1)} all-gather(bf16[384,48]{0,1:T(8,128)(2,1)S(1)} %copy-done.41), channel_id=1, replica_groups=mesh['dp'=16,'tensor'=2] {'dp'}, dimensions={1}, use_global_device_ids=true | all-gather | bytes 626688 | tf_op jit(solution)/shard_map/all_gather | solution.py:73
  129.1 7.4 add_convert_fusion
  138.2 145.9 %while.43 = (s32[]{:T(128)}, bf16[4,512,384]{2,1,0:T(8,128)(2,1)}, f32[4,6,512]{2,1,0:T(8,128)}, s32[4]{0:T(128)}, s32[2048]{0:T(1024)}, /*index=5*/s32[1,2048]{...) while((s32[]{:T(128)}, bf16[4,512,384]{2,1,0:T(8,128)(2,1)}, ...), condition=%wide.region_15.16_spmd, body=%wide.region_2.15_spmd.sunk | while | flops 1680012800 | bytes 86346096 | solution.py:124
  284.0 6.2 convolution_convert_fusion
  293.8 39.7 %reduce-scatter.12.cloned.1.call-done = bf16[1024,768]{1,0:T(8,128)(2,1)} async-done(((bf16[2048,768]{1,0:T(8,128)(2,1)}), bf16[1024,768]{1,0:T(8,128)(2,1)}) %reduce-scatter.12.cloned.1.call-update) | async-done | bytes 1572880 | tf_op jit(solution)/shard_map/reduce_scatter | solution.py:126
  340.2 38.0 %all-gather.17.cloned.1.call-done = bf16[1536,768]{0,1:T(8,128)(2,1)} async-done(((bf16[1536,48]{0,1:T(8,128)(2,1)}), bf16[1536,768]{0,1:T(8,128)(2,1)}) %all-gather.17.cloned.1.call-update) | async-done | bytes 2359312 | tf_op jit(solution)/shard_map/all_gather | solution.py:142
  381.0 42.4 %all-gather.19.cloned.1.call-done = bf16[2048,768]{1,0:T(8,128)(2,1)} async-done(((bf16[1024,768]{1,0:T(8,128)(2,1)}), bf16[2048,768]{1,0:T(8,128)(2,1)}) %all-gather.19.cloned.1.call-update) | async-done | bytes 3145744 | tf_op jit(solution)/shard_map/all_gather | solution.py:191
  423.4 44.7 %all-gather.15.cloned.1.call-done = bf16[768,1536]{1,0:T(8,128)(2,1)} async-done(((bf16[48,1536]{1,0:T(8,128)(2,1)}), bf16[768,1536]{1,0:T(8,128)(2,1)}) %all-gather.15.cloned.1.call-update) | async-done | bytes 2359312 | tf_op jit(solution)/shard_map/all_gather | solution.py:140
  468.2 45.9 %all-gather.13.cloned.1.call-done = bf16[2048,768]{1,0:T(8,128)(2,1)} async-done(((bf16[1024,768]{1,0:T(8,128)(2,1)}), bf16[2048,768]{1,0:T(8,128)(2,1)}) %all-gather.13.cloned.1.call-update) | async-done | bytes 3145744 | tf_op jit(solution)/shard_map/all_gather | solution.py:151
  514.1 47.8 %while.44 = (s32[]{:T(128)}, bf16[2,1024,1536]{2,1,0:T(8,128)(2,1)}, bf16[2,1024,1536]{2,1,0:T(8,128)(2,1)}, f32[2,1536]{1,0:T(2,128)S(1)}, s32[2]{0:T(128)S(1)}...) while((s32[]{:T(128)}, ...), condition=%wide.region_22.23_spmd, body=%wide.region_20.22_spmd.sunk | while | flops 4882168320 | bytes 102281512 | solution.py:203
  516.6 7.7 bitcast_dynamic-update-slice_fusion.7
  524.4 7.8 bitcast_dynamic-update-slice_fusion.8
  540.6 7.7 bitcast_dynamic-update-slice_fusion.7
  548.3 7.8 bitcast_dynamic-update-slice_fusion.8
  562.0 9.1 convolution_convert_fusion.1
  572.7 14.0 convolution_convert_fusion.2
  586.8 27.8 %reduce-scatter.16.cloned.1.call-done = bf16[1024,768]{1,0:T(8,128)(2,1)} async-done(((bf16[2048,768]{1,0:T(8,128)(2,1)}), bf16[1024,768]{1,0:T(8,128)(2,1)}) %reduce-scatter.16.cloned.1.call-update) | async-done | bytes 1572880 | tf_op jit(solution)/shard_map/reduce_scatter | solution.py:215
  614.6 3.9 fusion.146
  618.6 41.6 %reduce-scatter.14.cloned.1.call-done = bf16[1024,768]{1,0:T(8,128)(2,1)} async-done(((bf16[2048,768]{1,0:T(8,128)(2,1)}), bf16[1024,768]{1,0:T(8,128)(2,1)}) %reduce-scatter.14.cloned.1.call-update) | async-done | bytes 1572880 | tf_op jit(solution)/shard_map/reduce_scatter | solution.py:156
  660.2 4.6 fusion.161
  668.3 45.0 %all-gather.21.cloned.1.call-done = bf16[2048,768]{1,0:T(8,128)(2,1)} async-done(((bf16[1024,768]{1,0:T(8,128)(2,1)}), bf16[2048,768]{1,0:T(8,128)(2,1)}) %all-gather.21.cloned.1.call-update) | async-done | bytes 3145744 | tf_op jit(solution)/shard_map/all_gather | solution.py:230
  713.3 5.0 convolution_convert_fusion.3
  718.2 344.7 %while.45 = (s32[]{:T(128)}, f32[2048,384]{0,1:T(8,128)}, f32[2048,384]{0,1:T(8,128)}, bf16[4,512,384]{2,1,0:T(8,128)(2,1)}, s32[4]{0:T(128)}, /*index=5*/s32[20...) while((s32[]{:T(128)}, f32[2048,384]{0,1:T(8,128)}, ...), condition=%wide.region_33.34_spmd.clone, body=%wide.region_26.33_spmd.clone.sunk | while | flops 4111463936 | bytes 254159472 | solution.py:267
  734.2 4.7 multiply_reduce_fusion.14
  792.7 4.2 select_add_fusion.3
  816.3 4.7 multiply_reduce_fusion.14
  874.8 7.0 select_add_fusion.3
  901.1 4.7 multiply_reduce_fusion.14
  908.7 3.5 convolution_dynamic-update-slice_fusion.36
  959.6 7.0 select_add_fusion.3
  986.0 4.7 multiply_reduce_fusion.14
  1044.5 7.0 select_add_fusion.3
  1072.0 5.7 bitcast_convert_fusion
  1079.4 41.8 %reduce-scatter.18.cloned.1.call-done = bf16[1024,768]{1,0:T(8,128)(2,1)} async-done(((bf16[2048,768]{1,0:T(8,128)(2,1)}), bf16[1024,768]{1,0:T(8,128)(2,1)}) %reduce-scatter.18.cloned.1.call-update) | async-done | bytes 1572880 | tf_op jit(solution)/shard_map/reduce_scatter | solution.py:280
  1125.9 4.6 fusion.137
  1130.4 7.1 all-reduce.16
  1138.5 10.1 fusion.173
  1150.5 9.5 fusion.172
  1161.9 4.4 fusion.171
  1166.4 6.9 copy.50
  1173.3 8.4 fusion.135
  1183.0 60.1 %all-reduce.14 = (f32[768]{0:T(1024)S(1)}, f32[768]{0:T(1024)S(1)}, f32[768]{0:T(1024)S(1)}, f32[768]{0:T(1024)S(1)}, f32[768]{0:T(1024)S(1)}, /*index=5*/f32[3072]{0:T(1024)S(1)}, f32[768]{0:T(1024)S(1)}) all-reduce(bf16[768]{0:T(1024)(128)(2,1)S(1)} %get-tuple-element.392, ...), channel_id=6, replica_groups=mesh['dp'=16,'tensor'=2] {'dp'}, use_global_device_ids=true, to_apply=%region_39.40.clone | all-reduce | flops 7680 | bytes 46080
  1248.6 26.4 %reduce-scatter.26.cloned.1.call-done = f32[1536,48]{0,1:T(8,128)} async-done(((f32[1536,768]{0,1:T(8,128)}), f32[1536,48]{0,1:T(8,128)}) %reduce-scatter.26.cloned.1.call-update) | async-done | bytes 294928 | tf_op jit(solution)/shard_map/reduce_scatter | solution.py:213
  1275.1 78.9 %reduce-scatter.24.cloned.1.call-done = f32[48,1536]{1,0:T(8,128)} async-done(((f32[768,1536]{1,0:T(8,128)}), f32[48,1536]{1,0:T(8,128)}) %reduce-scatter.24.cloned.1.call-update) | async-done | bytes 294928 | tf_op jit(solution)/shard_map/reduce_scatter | solution.py:212
  1353.9 61.6 %reduce-scatter.22.cloned.1.call-done = f32[384,48]{0,1:T(8,128)} async-done(((f32[384,768]{0,1:T(8,128)}), f32[384,48]{0,1:T(8,128)}) %reduce-scatter.22.cloned.1.call-update) | async-done | bytes 73744 | tf_op jit(solution)/shard_map/reduce_scatter | solution.py:326
  1415.5 71.9 %reduce-scatter.20.cloned.1.call-done = f32[48,3,384]{2,0,1:T(8,128)} async-done(((f32[768,3,384]{2,0,1:T(8,128)}), f32[48,3,384]{2,0,1:T(8,128)}) %reduce-scatter.20.cloned.1.call-update) | async-done | bytes 221200 | tf_op jit(solution)/shard_map/reduce_scatter | solution.py:325
  (547 shorter events, 494.4 us)
Async XLA Ops:
  7.2 77.5 %copy-start = (bf16[1024,768]{1,0:T(8,128)(2,1)S(1)}, bf16[1024,768]{1,0:T(8,128)(2,1)}, u32[]{:S(2)}) copy-start(bf16[1024,768]{1,0:T(8,128)(2,1)} %param.21) | copy-start | bytes 4718596
  7.2 119.3 %all-gather.11.cloned.1.call-start = ((), (), s32[]{:S(2)}) async-start(), calls=%async_computation.10 | async-start | bytes 1880064 | tf_op jit(solution)/shard_map/all_gather | solution.py:71
  7.9 121.2 %all-gather.9.cloned.1.call-start = ((), (), s32[]{:S(2)}) async-start(), calls=%async_computation.9 | async-start | bytes 4718592 | tf_op jit(solution)/shard_map/all_gather | solution.py:85
  81.4 5.1 copy-start.50
  81.5 22.9 %copy-start.41 = (bf16[384,48]{0,1:T(8,128)(2,1)S(1)}, bf16[384,48]{0,1:T(8,128)(2,1)}, u32[]{:S(2)}) copy-start(bf16[384,48]{0,1:T(8,128)(2,1)} %param.27) | copy-start | bytes 110596
  86.5 246.9 %reduce-scatter.12.cloned.1.call-start = ((), (), s32[]{:S(2)}) async-start(), calls=%async_computation.11 | async-start | bytes 4718592 | tf_op jit(solution)/shard_map/reduce_scatter | solution.py:126
  284.0 6.2 copy-start.4
  284.0 6.2 copy-start.6
  290.3 43.2 %copy-start.1 = (bf16[1024,768]{1,0:T(8,128)(2,1)S(1)}, bf16[1024,768]{1,0:T(8,128)(2,1)}, u32[]{:S(2)}) copy-start(bf16[1024,768]{1,0:T(8,128)(2,1)} %param.21) | copy-start | bytes 4718596
  290.3 87.9 %all-gather.17.cloned.1.call-start = ((), (), s32[]{:S(2)}) async-start(), calls=%async_computation.14 | async-start | bytes 2506752 | tf_op jit(solution)/shard_map/all_gather | solution.py:142
  290.9 132.5 %all-gather.19.cloned.1.call-start = ((), (), s32[]{:S(2)}) async-start(), calls=%async_computation.16 | async-start | bytes 4718592 | tf_op jit(solution)/shard_map/all_gather | solution.py:191
  293.1 175.1 %all-gather.15.cloned.1.call-start = ((), (), s32[]{:S(2)}) async-start(), calls=%async_computation.13 | async-start | bytes 2506752 | tf_op jit(solution)/shard_map/all_gather | solution.py:140
  293.7 220.4 %all-gather.13.cloned.1.call-start = ((), (), s32[]{:S(2)}) async-start(), calls=%async_computation.12 | async-start | bytes 4718592 | tf_op jit(solution)/shard_map/all_gather | solution.py:151
  293.7 43.5 %copy-start.23 = (f32[768]{0:T(1024)}, f32[768]{0:T(1024)S(1)}, u32[]{:S(2)}) copy-start(f32[768]{0:T(1024)S(1)} %convert_element_type.220) | copy-start | bytes 9220
  293.8 43.5 %copy-start.31 = (f32[768]{0:T(1024)}, f32[768]{0:T(1024)S(1)}, u32[]{:S(2)}) copy-start(f32[768]{0:T(1024)S(1)} %convert_element_type.221) | copy-start | bytes 9220
  340.0 274.6 %reduce-scatter.16.cloned.1.call-start = ((), (), s32[]{:S(2)}) async-start(), calls=%async_computation.17 | async-start | bytes 4718592 | tf_op jit(solution)/shard_map/reduce_scatter | solution.py:215
  516.6 7.7 copy-start.52
  516.6 7.7 copy-start.55
  540.5 7.8 copy-start.52
  540.5 7.8 copy-start.55
  561.9 9.1 copy-start.42
  571.1 89.1 %reduce-scatter.14.cloned.1.call-start = ((), (), s32[]{:S(2)}) async-start(), calls=%async_computation.15 | async-start | bytes 4718592 | tf_op jit(solution)/shard_map/reduce_scatter | solution.py:156
  572.7 14.1 copy-start.46
  572.7 41.9 %copy-start.32 = (f32[768]{0:T(1024)S(1)}, f32[768]{0:T(1024)}, u32[]{:S(2)}) copy-start(f32[768]{0:T(1024)} %copy-done.31) | copy-start | bytes 9220
  572.7 41.9 %copy-start.34 = (f32[1024]{0:T(1024)S(1)}, f32[1024]{0:T(1024)}, u32[]{:S(2)}) copy-start(f32[1024]{0:T(1024)} %copy-done.33) | copy-start | bytes 12292
  586.7 27.9 %copy-start.2 = (bf16[1024,768]{1,0:T(8,128)(2,1)S(1)}, bf16[1024,768]{1,0:T(8,128)(2,1)}, u32[]{:S(2)}) copy-start(bf16[1024,768]{1,0:T(8,128)(2,1)} %param.21) | copy-start | bytes 4718596
  586.7 27.9 %copy-start.11 = (bf16[1024,768]{1,0:T(8,128)(2,1)S(1)}, bf16[1024,768]{1,0:T(8,128)(2,1)}, u32[]{:S(2)}) copy-start(bf16[1024,768]{1,0:T(8,128)(2,1)} %reduce-scatter.12.cloned.1.call-done) | copy-start | bytes 4718596
  586.7 27.9 %copy-start.24 = (f32[768]{0:T(1024)S(1)}, f32[768]{0:T(1024)}, u32[]{:S(2)}) copy-start(f32[768]{0:T(1024)} %copy-done.23) | copy-start | bytes 9220
  586.7 27.9 %copy-start.28 = (f32[1024]{0:T(1024)S(1)}, f32[1024]{0:T(1024)}, u32[]{:S(2)}) copy-start(f32[1024]{0:T(1024)} %copy-done.27) | copy-start | bytes 12292
  586.7 31.8 %copy-start.40 = (f32[1024]{0:T(1024)S(1)}, f32[1024]{0:T(1024)}, u32[]{:S(2)}) copy-start(f32[1024]{0:T(1024)} %copy-done.39) | copy-start | bytes 12292
  586.8 126.5 %all-gather.21.cloned.1.call-start = ((), (), s32[]{:S(2)}) async-start(), calls=%async_computation.18 | async-start | bytes 4718592 | tf_op jit(solution)/shard_map/all_gather | solution.py:230
  660.2 6.2 copy-start.16
  668.2 453.0 %reduce-scatter.18.cloned.1.call-start = ((), (), s32[]{:S(2)}) async-start(), calls=%async_computation.19 | async-start | bytes 4718592 | tf_op jit(solution)/shard_map/reduce_scatter | solution.py:280
  668.2 50.0 %copy-start.5 = (bf16[2048,384]{1,0:T(8,128)(2,1)S(1)}, bf16[2048,384]{1,0:T(8,128)(2,1)}, u32[]{:S(2)}) copy-start(bf16[2048,384]{1,0:T(8,128)(2,1)} %copy-done.4) | copy-start | bytes 4718596
  668.2 50.0 %copy-start.7 = (bf16[2048,384]{1,0:T(8,128)(2,1)S(1)}, bf16[2048,384]{1,0:T(8,128)(2,1)}, u32[]{:S(2)}) copy-start(bf16[2048,384]{1,0:T(8,128)(2,1)} %copy-done.6) | copy-start | bytes 4718596
  1072.0 5.8 copy-start.43
  1077.7 43.5 %copy-start.3 = (bf16[1024,768]{1,0:T(8,128)(2,1)S(1)}, bf16[1024,768]{1,0:T(8,128)(2,1)}, u32[]{:S(2)}) copy-start(bf16[1024,768]{1,0:T(8,128)(2,1)} %param.21) | copy-start | bytes 4718596
  1077.7 43.5 %copy-start.22 = (f32[1024]{0:T(1024)S(1)}, f32[1024]{0:T(1024)}, u32[]{:S(2)}) copy-start(f32[1024]{0:T(1024)} %copy-done.21) | copy-start | bytes 12292
  1077.7 43.5 %copy-start.26 = (f32[768]{0:T(1024)S(1)}, f32[768]{0:T(1024)}, u32[]{:S(2)}) copy-start(f32[768]{0:T(1024)} %copy-done.25) | copy-start | bytes 9220
  1077.7 45.9 %copy-start.38 = (f32[1024]{0:T(1024)S(1)}, f32[1024]{0:T(1024)}, u32[]{:S(2)}) copy-start(f32[1024]{0:T(1024)} %copy-done.37) | copy-start | bytes 12292
  1077.7 45.9 %copy-start.30 = (f32[1024]{0:T(1024)S(1)}, f32[1024]{0:T(1024)}, u32[]{:S(2)}) copy-start(f32[1024]{0:T(1024)} %copy-done.29) | copy-start | bytes 12292
  1077.7 169.5 %reduce-scatter.28.cloned.1.call-start = ((), (), s32[]{:S(2)}) async-start(), calls=%async_computation.24 | async-start | bytes 417792
  1125.9 4.6 copy-start.44
  1138.5 136.6 %reduce-scatter.26.cloned.1.call-start = ((), (), s32[]{:S(2)}) async-start(), calls=%async_computation.23 | async-start | bytes 5013504 | tf_op jit(solution)/shard_map/reduce_scatter | solution.py:213
  1148.6 205.3 %reduce-scatter.24.cloned.1.call-start = ((), (), s32[]{:S(2)}) async-start(), calls=%async_computation.22 | async-start | bytes 5013504 | tf_op jit(solution)/shard_map/reduce_scatter | solution.py:212
  1160.0 255.5 %reduce-scatter.22.cloned.1.call-start = ((), (), s32[]{:S(2)}) async-start(), calls=%async_computation.21 | async-start | bytes 1253376 | tf_op jit(solution)/shard_map/reduce_scatter | solution.py:326
  1166.3 7.0 copy-start.51
  1166.3 321.1 %reduce-scatter.20.cloned.1.call-start = ((), (), s32[]{:S(2)}) async-start(), calls=%async_computation.20 | async-start | bytes 3760128 | tf_op jit(solution)/shard_map/reduce_scatter | solution.py:325
  (37 other events, 72.5 us)
Sparse Core Ops, SparseCore 0:
  10.3 43.2 all-gather.10
  86.6 42.1 all-gather.8
  290.4 43.0 reduce-scatter.11
  335.8 42.3 all-gather.16
  379.7 43.7 all-gather.18
  425.8 42.3 all-gather.14
  470.3 43.7 all-gather.12
  571.2 43.3 reduce-scatter.15
  616.8 43.3 reduce-scatter.13
  668.3 44.9 all-gather.20
  1077.8 43.3 reduce-scatter.17
  1138.6 56.7 reduce-scatter.27
  1200.3 74.7 reduce-scatter.25
  1279.4 74.5 reduce-scatter.23
  1358.4 57.0 reduce-scatter.21
  1420.3 67.0 reduce-scatter.19
where the time goes:
time: 1500 us; the launch traced here: 1490 us
  waiting for transfers between devices  608 us (41%)
  matrix products  437 us (29%)
  blocking collectives  169 us (11%)
  other arithmetic  126 us (8%)
  local copies, waits for them, and re-layouts  107 us (7%)
  loops' own time  29.1 us (2%)
  between operations  17.5 us (1%)
    dot_general x77, matrix products, contract_cols(): lax.dot_general(left, right, (((1,), (1,)), ((), ())), preferred_element_...  205 us
    dot_general x52, matrix products, contract_rows(): lax.dot_general(left, right, (((0,), (0,)), ((), ())), preferred_element_...  126 us
    unnamed x2, blocking collectives  123 us
    reduce_scatter x1, waiting for transfers between devices, on_device(): lax.psum_scatter(d_fc_w, 'dp', scatter_dimension=0, tiled=True)  78.9 us
    reduce_scatter x1, waiting for transfers between devices, on_device(): lax.psum_scatter(d_qkv_w, 'dp', scatter_dimension=0, tiled=True)  71.9 us
    reduce_scatter x1, waiting for transfers between devices, on_device(): lax.psum_scatter(d_out_w, 'dp', scatter_dimension=1, tiled=True)  61.6 us
    all_gather x1, waiting for transfers between devices, on_device(): full_two = lax.all_gather(normed_two, 'tensor', axis=0, tiled=True)  45.9 us
    all_gather x1, waiting for transfers between devices, on_device(): lax.all_gather(scaled_mid.astype(jnp.bfloat16), 'tensor', axis=0, tiled=T...  45 us
  transfers between devices with their start and end apart: 16, of which 13 were waited for; matrix products, arithmetic and copies ran while one was open for 6% of the time, Pallas kernels for 0%

commit v1 on v0

--- a/solution.py
+++ b/solution.py
@@ -148,7 +148,15 @@
     normed_two = layer_norm(
         middle, gain_mlp.astype(jnp.float32), offset_mlp.astype(jnp.float32)
     ).astype(jnp.bfloat16)
-    full_two = lax.all_gather(normed_two, "tensor", axis=0, tiled=True)
+    ways, here = (lax.axis_size("tensor"), lax.axis_index("tensor"))
+    grown, reach = (normed_two, 1)
+    while reach < ways:
+        theirs = lax.ppermute(grown, "tensor", [(d, d ^ reach) for d in range(ways)])
+        mine_first = jnp.concatenate([grown, theirs], axis=0)
+        theirs_first = jnp.concatenate([theirs, grown], axis=0)
+        grown = jnp.where(here & reach == 0, mine_first, theirs_first)
+        reach = 2 * reach
+    full_two = grown
     inputs_rows = lax.slice_in_dim(full_two, 0, lax.axis_size("tensor") * local_rows, axis=0)
     activated = gelu_tanh(
         jnp.dot(inputs_rows, fc_weight, preferred_element_type=jnp.float32) + fc_bias

time: 1500 us -> 1460 us (0.973)
  waiting for transfers between devices: 608 us -> 557 us
    all_gather x1 -> x0, waiting for transfers between devices: 45.9 us -> none  [on_device(): full_two = lax.all_gather(normed_two, 'tensor', axis=0, tiled=True)]
  transfers between devices with their start and end apart: 16 -> 16, of which waited for: 13 -> 12; matrix products, arithmetic and copies ran while one was open for 6% -> 6% of each run, Pallas kernels for 0% -> 0%
where the time goes in v1:
time: 1460 us; the launch traced here: 1450 us
  waiting for transfers between devices  557 us (38%)
  matrix products  438 us (30%)
  blocking collectives  169 us (12%)
  other arithmetic  127 us (9%)
  local copies, waits for them, and re-layouts  108 us (7%)
  loops' own time  29 us (2%)
  between operations  17.4 us (1%)
    dot_general x77, matrix products, contract_cols(): lax.dot_general(left, right, (((1,), (1,)), ((), ())), preferred_element_...  205 us
    dot_general x52, matrix products, contract_rows(): lax.dot_general(left, right, (((0,), (0,)), ((), ())), preferred_element_...  126 us
    unnamed x2, blocking collectives  123 us
    reduce_scatter x1, waiting for transfers between devices, on_device(): lax.psum_scatter(d_fc_w, 'dp', scatter_dimension=0, tiled=True)  79 us
    reduce_scatter x1, waiting for transfers between devices, on_device(): lax.psum_scatter(d_qkv_w, 'dp', scatter_dimension=0, tiled=True)  71.9 us
    reduce_scatter x1, waiting for transfers between devices, on_device(): lax.psum_scatter(d_out_w, 'dp', scatter_dimension=1, tiled=True)  61.7 us
    all_gather x1, waiting for transfers between devices, on_device(): lax.all_gather(scaled_mid.astype(jnp.bfloat16), 'tensor', axis=0, tiled=T...  45 us
    all_gather x1, waiting for transfers between devices, on_device(): lax.all_gather(w_fc, 'dp', axis=0, tiled=True)  44.7 us
  transfers between devices with their start and end apart: 16, of which 12 were waited for; matrix products, arithmetic and copies ran while one was open for 6% of the time, Pallas kernels for 0%

profile of v1, /device:TPU:0, one launch (start us, length us, event | category | flops | bytes accessed | tf_op | source)
XLA Modules:
  0.0 1447.6 jit_solution(496923341558014517)
XLA Ops:
  16.5 63.2 %all-reduce.15 = (bf16[768]{0:T(1024)(128)(2,1)}, bf16[768]{0:T(1024)(128)(2,1)}, bf16[768]{0:T(1024)(128)(2,1)}, bf16[768]{0:T(1024)(128)(2,1)S(1)}, bf16[768]{...) all-reduce(bf16[768]{0:T(1024)(128)(2,1)S(1)} %dynamic-update-slice, ...), channel_id=1, replica_groups=mesh['dp'=16,'tensor'=2] {'dp'}, use_global_device_ids=true, to_apply=%add.4 | all-reduce | flops 7680 | bytes 30720
  86.6 17.0 %all-gather = bf16[16,48,2]{1,2,0:T(2,128)(2,1)S(1)} all-gather(bf16[1,48,2]{1,2,0:T(2,128)(2,1)S(1)} %bitcast.226), channel_id=1, replica_groups=mesh['dp'=16,'tensor'=2] {'dp'}, dimensions={0}, use_global_device_ids=true | all-gather | bytes 3264 | tf_op jit(solution)/shard_map/all_gather | solution.py:72
  104.4 22.1 %all_gather.57 = bf16[384,768]{0,1:T(8,128)(2,1)} all-gather(bf16[384,48]{0,1:T(8,128)(2,1)S(1)} %copy-done.43), channel_id=1, replica_groups=mesh['dp'=16,'tensor'=2] {'dp'}, dimensions={1}, use_global_device_ids=true | all-gather | bytes 626688 | tf_op jit(solution)/shard_map/all_gather | solution.py:73
  129.1 7.4 add_convert_fusion
  138.1 145.9 %while.43 = (s32[]{:T(128)}, bf16[4,512,384]{2,1,0:T(8,128)(2,1)}, f32[4,6,512]{2,1,0:T(8,128)}, s32[4]{0:T(128)}, s32[2048]{0:T(1024)}, /*index=5*/s32[1,2048]{...) while((s32[]{:T(128)}, bf16[4,512,384]{2,1,0:T(8,128)(2,1)}, ...), condition=%wide.region_15.16_spmd, body=%wide.region_2.15_spmd.sunk | while | flops 1680012800 | bytes 86346096 | solution.py:124
  284.0 6.2 convolution_convert_fusion
  293.8 39.6 %reduce-scatter.12.cloned.1.call-done = bf16[1024,768]{1,0:T(8,128)(2,1)} async-done(((bf16[2048,768]{1,0:T(8,128)(2,1)}), bf16[1024,768]{1,0:T(8,128)(2,1)}) %reduce-scatter.12.cloned.1.call-update) | async-done | bytes 1572880 | tf_op jit(solution)/shard_map/reduce_scatter | solution.py:126
  338.8 39.4 %all-gather.14.cloned.1.call-done = bf16[1536,768]{0,1:T(8,128)(2,1)} async-done(((bf16[1536,48]{0,1:T(8,128)(2,1)}), bf16[1536,768]{0,1:T(8,128)(2,1)}) %all-gather.14.cloned.1.call-update) | async-done | bytes 2359312 | tf_op jit(solution)/shard_map/all_gather | solution.py:142
  378.2 4.3 copy.46
  384.6 39.4 %all-gather.16.cloned.1.call-done = bf16[2048,768]{1,0:T(8,128)(2,1)} async-done(((bf16[1024,768]{1,0:T(8,128)(2,1)}), bf16[2048,768]{1,0:T(8,128)(2,1)}) %all-gather.16.cloned.1.call-update) | async-done | bytes 3145744 | tf_op jit(solution)/shard_map/all_gather | solution.py:199
  424.0 44.7 %all-gather.12.cloned.1.call-done = bf16[768,1536]{1,0:T(8,128)(2,1)} async-done(((bf16[48,1536]{1,0:T(8,128)(2,1)}), bf16[768,1536]{1,0:T(8,128)(2,1)}) %all-gather.12.cloned.1.call-update) | async-done | bytes 2359312 | tf_op jit(solution)/shard_map/all_gather | solution.py:140
  468.7 47.9 %while.44 = (s32[]{:T(128)}, bf16[2,1024,1536]{2,1,0:T(8,128)(2,1)}, bf16[2,1024,1536]{2,1,0:T(8,128)(2,1)}, f32[2,1536]{1,0:T(2,128)S(1)}, s32[2]{0:T(128)S(1)}...) while((s32[]{:T(128)}, ...), condition=%wide.region_22.23_spmd, body=%wide.region_20.22_spmd.sunk | while | flops 4882168320 | bytes 111718728 | solution.py:211
  471.3 7.7 bitcast_dynamic-update-slice_fusion.7
  479.0 7.8 bitcast_dynamic-update-slice_fusion.8
  495.2 7.7 bitcast_dynamic-update-slice_fusion.7
  503.0 7.8 bitcast_dynamic-update-slice_fusion.8
  516.6 9.1 convolution_convert_fusion.1
  527.6 15.3 %convolution_convert_fusion.2 = bf16[2048,768]{1,0:T(8,128)(2,1)} fusion(bf16[1536,768]{0,1:T(8,128)(2,1)} %all-gather.14.cloned.1.call-done, bf16[2048,768]{1,0:T(8,128)(2,1)S(1)} %copy-done.19, bf16[768,1536]{1,0:T(8,128)(2,1)} %get-tuple-element.944, f32[1536]{0:T(1024)S(1)} %get-tuple-element.938), kind=kOutput, calls=%fused_computation.239 | convolution fusion | flops 9696706560 | bytes 11016192 | tf_op jit(solution)/shard_map/dot_general | solution.py:165
  543.5 24.6 %reduce-scatter.16.cloned.1.call-done = bf16[1024,768]{1,0:T(8,128)(2,1)} async-done(((bf16[2048,768]{1,0:T(8,128)(2,1)}), bf16[1024,768]{1,0:T(8,128)(2,1)}) %reduce-scatter.16.cloned.1.call-update) | async-done | bytes 1572880 | tf_op jit(solution)/shard_map/reduce_scatter | solution.py:223
  568.1 3.8 fusion.146
  571.9 41.8 %reduce-scatter.14.cloned.1.call-done = bf16[1024,768]{1,0:T(8,128)(2,1)} async-done(((bf16[2048,768]{1,0:T(8,128)(2,1)}), bf16[1024,768]{1,0:T(8,128)(2,1)}) %reduce-scatter.14.cloned.1.call-update) | async-done | bytes 1572880 | tf_op jit(solution)/shard_map/reduce_scatter | solution.py:164
  613.7 4.6 fusion.161
  621.7 45.0 %all-gather.18.cloned.1.call-done = bf16[2048,768]{1,0:T(8,128)(2,1)} async-done(((bf16[1024,768]{1,0:T(8,128)(2,1)}), bf16[2048,768]{1,0:T(8,128)(2,1)}) %all-gather.18.cloned.1.call-update) | async-done | bytes 3145744 | tf_op jit(solution)/shard_map/all_gather | solution.py:238
  666.7 5.0 convolution_convert_fusion.3
  671.7 344.6 %while.45 = (s32[]{:T(128)}, f32[2048,384]{0,1:T(8,128)}, f32[2048,384]{0,1:T(8,128)}, bf16[4,512,384]{2,1,0:T(8,128)(2,1)}, s32[4]{0:T(128)}, /*index=5*/s32[20...) while((s32[]{:T(128)}, f32[2048,384]{0,1:T(8,128)}, ...), condition=%wide.region_33.34_spmd.clone, body=%wide.region_26.33_spmd.clone.sunk | while | flops 4111463936 | bytes 254159472 | solution.py:275
  687.5 4.7 multiply_reduce_fusion.14
  746.0 4.2 select_add_fusion.3
  769.6 4.7 multiply_reduce_fusion.14
  828.1 7.0 select_add_fusion.3
  854.4 4.7 multiply_reduce_fusion.14
  862.0 3.5 convolution_dynamic-update-slice_fusion.36
  912.9 7.0 select_add_fusion.3
  939.3 4.7 multiply_reduce_fusion.14
  997.8 7.0 select_add_fusion.3
  1025.3 5.7 bitcast_convert_fusion
  1032.7 41.8 %reduce-scatter.18.cloned.1.call-done = bf16[1024,768]{1,0:T(8,128)(2,1)} async-done(((bf16[2048,768]{1,0:T(8,128)(2,1)}), bf16[1024,768]{1,0:T(8,128)(2,1)}) %reduce-scatter.18.cloned.1.call-update) | async-done | bytes 1572880 | tf_op jit(solution)/shard_map/reduce_scatter | solution.py:288
  1079.2 4.6 fusion.137
  1083.8 7.1 all-reduce.16
  1091.9 10.1 fusion.173
  1103.8 9.5 fusion.172
  1115.2 4.3 fusion.171
  1119.7 6.9 copy.50
  1126.6 8.4 fusion.135
  1136.3 60.0 %all-reduce.14 = (f32[768]{0:T(1024)S(1)}, f32[768]{0:T(1024)S(1)}, f32[768]{0:T(1024)S(1)}, f32[768]{0:T(1024)S(1)}, f32[768]{0:T(1024)S(1)}, /*index=5*/f32[3072]{0:T(1024)S(1)}, f32[768]{0:T(1024)S(1)}) all-reduce(bf16[768]{0:T(1024)(128)(2,1)S(1)} %get-tuple-element.392, ...), channel_id=6, replica_groups=mesh['dp'=16,'tensor'=2] {'dp'}, use_global_device_ids=true, to_apply=%region_39.40.clone | all-reduce | flops 7680 | bytes 46080
  1201.8 26.5 %reduce-scatter.26.cloned.1.call-done = f32[1536,48]{0,1:T(8,128)} async-done(((f32[1536,768]{0,1:T(8,128)}), f32[1536,48]{0,1:T(8,128)}) %reduce-scatter.26.cloned.1.call-update) | async-done | bytes 294928 | tf_op jit(solution)/shard_map/reduce_scatter | solution.py:221
  1228.3 79.0 %reduce-scatter.24.cloned.1.call-done = f32[48,1536]{1,0:T(8,128)} async-done(((f32[768,1536]{1,0:T(8,128)}), f32[48,1536]{1,0:T(8,128)}) %reduce-scatter.24.cloned.1.call-update) | async-done | bytes 294928 | tf_op jit(solution)/shard_map/reduce_scatter | solution.py:220
  1307.3 61.7 %reduce-scatter.22.cloned.1.call-done = f32[384,48]{0,1:T(8,128)} async-done(((f32[384,768]{0,1:T(8,128)}), f32[384,48]{0,1:T(8,128)}) %reduce-scatter.22.cloned.1.call-update) | async-done | bytes 73744 | tf_op jit(solution)/shard_map/reduce_scatter | solution.py:334
  1369.0 71.9 %reduce-scatter.20.cloned.1.call-done = f32[48,3,384]{2,0,1:T(8,128)} async-done(((f32[768,3,384]{2,0,1:T(8,128)}), f32[48,3,384]{2,0,1:T(8,128)}) %reduce-scatter.20.cloned.1.call-update) | async-done | bytes 221200 | tf_op jit(solution)/shard_map/reduce_scatter | solution.py:333
  (551 shorter events, 493.0 us)
Async XLA Ops:
  7.2 77.5 %copy-start = (bf16[1024,768]{1,0:T(8,128)(2,1)S(1)}, bf16[1024,768]{1,0:T(8,128)(2,1)}, u32[]{:S(2)}) copy-start(bf16[1024,768]{1,0:T(8,128)(2,1)} %param.21) | copy-start | bytes 4718596
  7.2 119.3 %all-gather.10.cloned.1.call-start = ((), (), s32[]{:S(2)}) async-start(), calls=%async_computation.10 | async-start | bytes 1880064 | tf_op jit(solution)/shard_map/all_gather | solution.py:71
  7.9 121.2 %all-gather.8.cloned.1.call-start = ((), (), s32[]{:S(2)}) async-start(), calls=%async_computation.9 | async-start | bytes 4718592 | tf_op jit(solution)/shard_map/all_gather | solution.py:85
  81.5 22.9 %copy-start.43 = (bf16[384,48]{0,1:T(8,128)(2,1)S(1)}, bf16[384,48]{0,1:T(8,128)(2,1)}, u32[]{:S(2)}) copy-start(bf16[384,48]{0,1:T(8,128)(2,1)} %param.27) | copy-start | bytes 110596
  86.5 246.9 %reduce-scatter.12.cloned.1.call-start = ((), (), s32[]{:S(2)}) async-start(), calls=%async_computation.11 | async-start | bytes 4718592 | tf_op jit(solution)/shard_map/reduce_scatter | solution.py:126
  284.0 6.2 copy-start.4
  284.0 6.2 copy-start.6
  290.3 43.2 %copy-start.1 = (bf16[1024,768]{1,0:T(8,128)(2,1)S(1)}, bf16[1024,768]{1,0:T(8,128)(2,1)}, u32[]{:S(2)}) copy-start(bf16[1024,768]{1,0:T(8,128)(2,1)} %param.21) | copy-start | bytes 4718596
  290.3 87.9 %all-gather.14.cloned.1.call-start = ((), (), s32[]{:S(2)}) async-start(), calls=%async_computation.13 | async-start | bytes 2506752 | tf_op jit(solution)/shard_map/all_gather | solution.py:142
  290.9 133.1 %all-gather.16.cloned.1.call-start = ((), (), s32[]{:S(2)}) async-start(), calls=%async_computation.15 | async-start | bytes 4718592 | tf_op jit(solution)/shard_map/all_gather | solution.py:199
  293.1 175.6 %all-gather.12.cloned.1.call-start = ((), (), s32[]{:S(2)}) async-start(), calls=%async_computation.12 | async-start | bytes 2506752 | tf_op jit(solution)/shard_map/all_gather | solution.py:140
  293.7 274.4 %reduce-scatter.16.cloned.1.call-start = ((), (), s32[]{:S(2)}) async-start(), calls=%async_computation.16 | async-start | bytes 4718592 | tf_op jit(solution)/shard_map/reduce_scatter | solution.py:223
  293.8 43.5 %copy-start.25 = (f32[768]{0:T(1024)}, f32[768]{0:T(1024)S(1)}, u32[]{:S(2)}) copy-start(f32[768]{0:T(1024)S(1)} %convert_element_type.220) | copy-start | bytes 9220
  293.8 43.5 %copy-start.33 = (f32[768]{0:T(1024)}, f32[768]{0:T(1024)S(1)}, u32[]{:S(2)}) copy-start(f32[768]{0:T(1024)S(1)} %convert_element_type.221) | copy-start | bytes 9220
  338.3 44.2 %collective-permute-start = (bf16[1024,768]{1,0:T(8,128)(2,1)S(1)}, bf16[1024,768]{1,0:T(8,128)(2,1)S(1)}, u32[]{:S(2)}, u32[]{:S(2)}) collective-permute-start(bf16[1024,768]{1,0:T(8,128)(2,1)S(1)} %add_convert_fusion.3), channel_id=1, source_target_pairs={{0,1},{1,0},{2,3},{3,2},{4,5},{5,4},{6,7},{7,6},{8,9},{9,8},{10,11... | collective-permute-start | bytes 4718600 | tf_op jit(solution)/shard_map/ppermute | solution.py:154
  471.3 7.7 copy-start.21
  471.3 7.7 copy-start.54
  471.3 7.7 copy-start.56
  495.2 7.8 copy-start.21
  495.2 7.8 copy-start.54
  495.2 7.8 copy-start.56
  516.6 9.1 copy-start.44
  525.8 87.9 %reduce-scatter.14.cloned.1.call-start = ((), (), s32[]{:S(2)}) async-start(), calls=%async_computation.14 | async-start | bytes 4718592 | tf_op jit(solution)/shard_map/reduce_scatter | solution.py:164
  527.6 15.8 %copy-start.48 = (bf16[768]{0:T(1024)(128)(2,1)S(1)}, bf16[768]{0:T(1024)(128)(2,1)}, u32[]{:S(2)}) copy-start(bf16[768]{0:T(1024)(128)(2,1)} %get-tuple-element.391) | copy-start | bytes 4612
  527.6 40.5 %copy-start.34 = (f32[768]{0:T(1024)S(1)}, f32[768]{0:T(1024)}, u32[]{:S(2)}) copy-start(f32[768]{0:T(1024)} %copy-done.33) | copy-start | bytes 9220
  527.6 40.5 %copy-start.36 = (f32[1024]{0:T(1024)S(1)}, f32[1024]{0:T(1024)}, u32[]{:S(2)}) copy-start(f32[1024]{0:T(1024)} %copy-done.35) | copy-start | bytes 12292
  543.0 25.1 %copy-start.2 = (bf16[1024,768]{1,0:T(8,128)(2,1)S(1)}, bf16[1024,768]{1,0:T(8,128)(2,1)}, u32[]{:S(2)}) copy-start(bf16[1024,768]{1,0:T(8,128)(2,1)} %param.21) | copy-start | bytes 4718596
  543.0 25.1 %copy-start.11 = (bf16[1024,768]{1,0:T(8,128)(2,1)S(1)}, bf16[1024,768]{1,0:T(8,128)(2,1)}, u32[]{:S(2)}) copy-start(bf16[1024,768]{1,0:T(8,128)(2,1)} %reduce-scatter.12.cloned.1.call-done) | copy-start | bytes 4718596
  543.0 25.1 %copy-start.26 = (f32[768]{0:T(1024)S(1)}, f32[768]{0:T(1024)}, u32[]{:S(2)}) copy-start(f32[768]{0:T(1024)} %copy-done.25) | copy-start | bytes 9220
  543.0 25.1 %copy-start.30 = (f32[1024]{0:T(1024)S(1)}, f32[1024]{0:T(1024)}, u32[]{:S(2)}) copy-start(f32[1024]{0:T(1024)} %copy-done.29) | copy-start | bytes 12292
  543.0 28.9 %copy-start.42 = (f32[1024]{0:T(1024)S(1)}, f32[1024]{0:T(1024)}, u32[]{:S(2)}) copy-start(f32[1024]{0:T(1024)} %copy-done.41) | copy-start | bytes 12292
  543.0 123.7 %all-gather.18.cloned.1.call-start = ((), (), s32[]{:S(2)}) async-start(), calls=%async_computation.17 | async-start | bytes 4718592 | tf_op jit(solution)/shard_map/all_gather | solution.py:238
  613.7 6.2 copy-start.16
  621.6 452.9 %reduce-scatter.18.cloned.1.call-start = ((), (), s32[]{:S(2)}) async-start(), calls=%async_computation.18 | async-start | bytes 4718592 | tf_op jit(solution)/shard_map/reduce_scatter | solution.py:288
  621.7 50.0 %copy-start.5 = (bf16[2048,384]{1,0:T(8,128)(2,1)S(1)}, bf16[2048,384]{1,0:T(8,128)(2,1)}, u32[]{:S(2)}) copy-start(bf16[2048,384]{1,0:T(8,128)(2,1)} %copy-done.4) | copy-start | bytes 4718596
  621.7 50.0 %copy-start.7 = (bf16[2048,384]{1,0:T(8,128)(2,1)S(1)}, bf16[2048,384]{1,0:T(8,128)(2,1)}, u32[]{:S(2)}) copy-start(bf16[2048,384]{1,0:T(8,128)(2,1)} %copy-done.6) | copy-start | bytes 4718596
  1025.3 5.8 copy-start.45
  1031.0 43.6 %copy-start.3 = (bf16[1024,768]{1,0:T(8,128)(2,1)S(1)}, bf16[1024,768]{1,0:T(8,128)(2,1)}, u32[]{:S(2)}) copy-start(bf16[1024,768]{1,0:T(8,128)(2,1)} %param.21) | copy-start | bytes 4718596
  1031.0 43.6 %copy-start.24 = (f32[1024]{0:T(1024)S(1)}, f32[1024]{0:T(1024)}, u32[]{:S(2)}) copy-start(f32[1024]{0:T(1024)} %copy-done.23) | copy-start | bytes 12292
  1031.0 43.6 %copy-start.28 = (f32[768]{0:T(1024)S(1)}, f32[768]{0:T(1024)}, u32[]{:S(2)}) copy-start(f32[768]{0:T(1024)} %copy-done.27) | copy-start | bytes 9220
  1031.0 45.9 %copy-start.40 = (f32[1024]{0:T(1024)S(1)}, f32[1024]{0:T(1024)}, u32[]{:S(2)}) copy-start(f32[1024]{0:T(1024)} %copy-done.39) | copy-start | bytes 12292
  1031.0 45.9 %copy-start.32 = (f32[1024]{0:T(1024)S(1)}, f32[1024]{0:T(1024)}, u32[]{:S(2)}) copy-start(f32[1024]{0:T(1024)} %copy-done.31) | copy-start | bytes 12292
  1031.0 169.4 %reduce-scatter.28.cloned.1.call-start = ((), (), s32[]{:S(2)}) async-start(), calls=%async_computation.23 | async-start | bytes 417792
  1091.8 136.5 %reduce-scatter.26.cloned.1.call-start = ((), (), s32[]{:S(2)}) async-start(), calls=%async_computation.22 | async-start | bytes 5013504 | tf_op jit(solution)/shard_map/reduce_scatter | solution.py:221
  1101.9 205.4 %reduce-scatter.24.cloned.1.call-start = ((), (), s32[]{:S(2)}) async-start(), calls=%async_computation.21 | async-start | bytes 5013504 | tf_op jit(solution)/shard_map/reduce_scatter | solution.py:220
  1113.4 255.6 %reduce-scatter.22.cloned.1.call-start = ((), (), s32[]{:S(2)}) async-start(), calls=%async_computation.20 | async-start | bytes 1253376 | tf_op jit(solution)/shard_map/reduce_scatter | solution.py:334
  1119.6 7.0 copy-start.53
  1119.6 321.2 %reduce-scatter.20.cloned.1.call-start = ((), (), s32[]{:S(2)}) async-start(), calls=%async_computation.19 | async-start | bytes 3760128 | tf_op jit(solution)/shard_map/reduce_scatter | solution.py:333
  (39 other events, 83.1 us)
Sparse Core Ops, SparseCore 0:
  10.3 43.2 all-gather.9
  86.6 42.1 all-gather.7
  290.4 43.0 reduce-scatter.11
  335.8 42.3 all-gather.13
  380.2 43.7 all-gather.15
  426.4 42.3 all-gather.11
  525.9 42.1 reduce-scatter.15
  570.3 43.3 reduce-scatter.13
  621.7 44.9 all-gather.17
  1031.1 43.3 reduce-scatter.17
  1091.9 56.7 reduce-scatter.27
  1153.5 74.7 reduce-scatter.25
  1232.7 74.5 reduce-scatter.23
  1311.8 57.1 reduce-scatter.21
  1373.8 67.0 reduce-scatter.19
